TPU v7x, 128 devices: a whole 4x4x4 slice. The times are simulated.
128 devices in a mesh: grp: 4 (over y), col: 32 (over x, z, core).
Axes of the slice: x: 4, y: 4, z: 4, core: 2. Of those that a mesh axis runs over, the one named last changes fastest.
Arguments:
- blocks: bfloat16 [24576, 32, 1024], P(('grp', 'col'))
- i_index: int32 [24576], P(('grp', 'col')), may hold values from 0 to 63
- j_index: int32 [24576], P(('grp', 'col')), may hold values from 0 to 63
- k_index: int32 [24576], P(('grp', 'col')), may hold values from 0 to 15
- block_count: int32 [128], P(('grp', 'col')), may hold values from 24 to 192, as said below
- b_factor: float32 [65536, 256], P(('grp', 'col'))
- c_factor: float32 [16384, 256], P(('grp', 'col'))
Outputs:
- a_update: float32 [8192, 256], P(('grp', 'col'))
- b_update: float32 [65536, 256], P(('grp', 'col'))
Inputs may be any that keep to these rules, and one draw needn't show every extreme that they name: block_count[d] is the number of live slots of device d = 32 * (grp index) + (col index): its slots d * 192 to d * 192 + block_count[d] - 1; every other slot is ignored. Some device has exactly 192 live slots.
All inputs are finite; a program needn't handle non-finite values.
Results may differ from a plain program's by a relative error of at most 0.005.
The roundings to bfloat16 on the way count: a program that leaves them out, or rounds other values in their place, can miss the bound.
Values may be sent and summed in bfloat16 or wider, within the bound.
No kernel may reach another device: no remote copies, remote signals or barrier semaphores. Data moves between devices by JAX's collectives and lax.ppermute only.
A program may use at most 128 MiB of HBM per device.

v0:
```python
import jax
import jax.numpy as jnp
from jax import lax
from jax.sharding import PartitionSpec as P

A_DEV = 2


def solve_rows(gram, right_side):
    factor_low = lax.linalg.cholesky(gram)
    halfway = lax.linalg.triangular_solve(
        factor_low, right_side, left_side=False, lower=True, transpose_a=True
    )
    return lax.linalg.triangular_solve(
        factor_low, halfway, left_side=False, lower=True, transpose_a=False
    )


def mode_term(
    blocks,
    left_rows,
    left_index,
    tail_rows,
    tail_index,
    target_index,
    live_mask,
    targets,
    first_mode,
):
    block_edge = blocks.shape[1]
    rank_width = left_rows.shape[1]
    group_size = 16
    groups = blocks.shape[0] // group_size
    left_table = left_rows.reshape(-1, block_edge, rank_width)
    tail_table = tail_rows.reshape(-1, block_edge, rank_width)
    target_ids = jnp.arange(targets, dtype=jnp.int32)

    def one_step(running, inputs):
        tensor_group, left_idx, tail_idx, target_idx, alive_row = inputs
        left_blk = left_table[left_idx].astype(jnp.float32)
        tail_blk = tail_table[tail_idx].astype(jnp.float32)
        product = (left_blk[:, :, None, :] * tail_blk[:, None, :, :]).astype(jnp.bfloat16)
        if first_mode:
            result = jnp.einsum(
                "bim,bmr->bir",
                tensor_group,
                product.reshape(group_size, block_edge * block_edge, rank_width),
                preferred_element_type=jnp.float32,
            )
        else:
            result = jnp.einsum(
                "bijk,bikr->bjr",
                tensor_group.reshape(group_size, block_edge, block_edge, block_edge),
                product,
                preferred_element_type=jnp.float32,
            )
        select = (target_idx[None, :] == target_ids[:, None]).astype(jnp.float32) * alive_row[
            None, :
        ]
        update = jnp.dot(
            select,
            result.reshape(group_size, block_edge * rank_width),
            precision=lax.Precision.HIGHEST,
        )
        return (running + update, None)

    inputs = (
        blocks.reshape(groups, group_size, block_edge, block_edge * block_edge),
        left_index.reshape(groups, group_size),
        tail_index.reshape(groups, group_size),
        target_index.reshape(groups, group_size),
        live_mask.reshape(groups, group_size),
    )
    start_value = jnp.zeros((targets, block_edge * rank_width), jnp.float32)
    running, _ = lax.scan(one_step, start_value, inputs)
    return running.reshape(targets * block_edge, rank_width)


def on_device(blocks, i_index, j_index, k_index, block_count, b_factor, c_factor):
    highest = lax.Precision.HIGHEST
    block_edge = blocks.shape[1]
    gram_second, gram_third = lax.psum(
        (
            jnp.dot(b_factor.T, b_factor, precision=highest),
            jnp.dot(c_factor.T, c_factor, precision=highest),
        ),
        ("grp", "col"),
    )
    b_range, c_range = (
        lax.all_gather(b_factor.astype(jnp.bfloat16), "grp", axis=0, tiled=True),
        lax.all_gather(c_factor.astype(jnp.bfloat16), "grp", axis=0, tiled=True),
    )
    live_mask = (jnp.arange(blocks.shape[0], dtype=jnp.int32) < block_count[0]).astype(jnp.float32)
    first_targets = A_DEV * lax.axis_size("col")
    second_targets = b_range.shape[0] // block_edge
    partial_value = mode_term(
        blocks, b_range, j_index, c_range, k_index, i_index, live_mask, first_targets, True
    )
    gram_one = gram_second * gram_third
    whole_sum = lax.psum(partial_value, "col")
    a_whole = solve_rows(gram_one, whole_sum)
    gram_first = lax.psum(jnp.dot(a_whole.T, a_whole, precision=highest), "grp")
    col_norm = jnp.sqrt(jnp.diagonal(gram_first) + 1e-06)
    a_range = (a_whole / col_norm[None, :]).astype(jnp.bfloat16)
    own_rows = A_DEV * block_edge
    a_update = lax.dynamic_slice_in_dim(a_whole, lax.axis_index("col") * own_rows, own_rows, 0)
    gram_two = gram_first / (col_norm[:, None] * col_norm[None, :]) * gram_third
    partial_two = mode_term(
        blocks, a_range, i_index, c_range, k_index, j_index, live_mask, second_targets, False
    )
    own_two = lax.psum_scatter(partial_two, "grp", scatter_dimension=0, tiled=True)
    b_update = solve_rows(gram_two, own_two)
    return (a_update, b_update)


def solution(mesh):
    return jax.shard_map(
        on_device,
        mesh=mesh,
        in_specs=(
            P(("grp", "col"), None, None),
            P(("grp", "col")),
            P(("grp", "col")),
            P(("grp", "col")),
            P(("grp", "col")),
            P(("grp", "col"), None),
            P(("grp", "col"), None),
        ),
        out_specs=(P(("grp", "col"), None), P(("grp", "col"), None)),
        check_vma=False,
    )
```

profile of v0, /device:TPU:0, one launch (start us, length us, event | category | flops | bytes accessed | tf_op | source)
XLA Modules:
  0.0 780.1 jit_solution(10742429783290168959)
XLA Ops:
  8.1 2.9 fusion.61
  15.0 13.0 %all_gather.7 = bf16[512,256]{1,0:T(8,128)(2,1)S(1)} all-gather(bf16[128,256]{1,0:T(8,128)(2,1)S(1)} %convert_element_type.56), channel_id=1, replica_groups=mesh['grp'=4,'col'=32] {'grp'}, dimensions={0}, use_global_device_ids=true | all-gather | bytes 327680 | tf_op jit(solution)/shard_map/all_gather | solution.py:91
  28.0 135.6 %all-reduce.10.cloned.1.call-done = (f32[256,256]{0,1:T(8,128)}, f32[256,256]{0,1:T(8,128)}) async-done(((f32[256,256]{0,1:T(8,128)}, f32[256,256]{0,1:T(8,128)}), (f32[256,256]{0,1:T(8,128)}, f32[256,256]{0,1:T(8,128)})) %all-reduce.10.cloned.1.call-update) | async-done | bytes 524304 | tf_op jit(solution)/shard_map/psum | solution.py:82
  164.8 11.7 %custom-call.29 = f32[128,128]{1,0:T(8,128)S(1)} custom-call(f32[128,128]{1,0:T(8,128)S(1)} %slice.101), custom_call_target="Cholesky" | custom-call | tf_op jit(solution)/shard_map/cholesky/custom-call.2 | solution.py:10
  176.6 9.8 %custom-call.30 = f32[1,128,128]{1,2,0:T(8,128)S(1)} custom-call(f32[1,128,128]{2,1,0:T(8,128)S(1)} %get-tuple-element.262), custom_call_target="InvertDiagBlocksLowerTriangular" | custom-call | tf_op jit(solution)/shard_map/cholesky/custom-call.7 | solution.py:10
  187.1 11.7 %custom-call.31 = f32[128,128]{1,0:T(8,128)S(1)} custom-call(f32[128,128]{1,0:T(8,128)S(1)} %convolution_subtract_fusion.5), custom_call_target="Cholesky" | custom-call | tf_op jit(solution)/shard_map/cholesky/custom-call.3 | solution.py:10
  198.9 141.3 %while.26 = (s32[]{:T(128)}, f32[64,8192]{1,0:T(8,128)S(1)}, s32[12,16]{1,0:T(8,128)S(1)}, f32[12,16]{1,0:T(8,128)S(1)}, bf16[12,16,32,1024]{3,2,1,0:T(8,128)(2,...) while((s32[]{:T(128)}, f32[64,8192]{1,0:T(8,128)S(1)}, ...), condition=%wide.region_1.0_spmd.clone, body=%wide.region_0.0_spmd.clone.sunk | while | flops 378802272 | bytes 27796492 | solution.py:75
  201.6 3.9 multiply_convert_fusion.5
  205.4 2.7 fusion.109
  213.3 3.9 multiply_convert_fusion.5
  225.1 3.9 multiply_convert_fusion.5
  228.9 2.7 fusion.109
  236.8 3.9 multiply_convert_fusion.5
  240.7 2.7 fusion.109
  248.6 3.9 multiply_convert_fusion.5
  252.5 2.7 fusion.109
  260.4 3.9 multiply_convert_fusion.5
  264.2 2.7 fusion.109
  272.1 3.9 multiply_convert_fusion.5
  276.0 2.7 fusion.109
  283.9 3.9 multiply_convert_fusion.5
  287.8 2.7 fusion.109
  295.7 3.9 multiply_convert_fusion.5
  299.5 2.7 fusion.109
  307.4 3.9 multiply_convert_fusion.5
  311.3 2.7 fusion.109
  319.2 3.9 multiply_convert_fusion.5
  323.1 2.7 fusion.109
  331.0 3.9 multiply_convert_fusion.5
  344.0 4.3 while.24
  348.3 19.7 %custom-call.20 = f32[2,128,128]{1,2,0:T(8,128)S(1)} custom-call(f32[2,128,128]{2,1,0:T(8,128)S(1)} %get-tuple-element.116), custom_call_target="InvertDiagBlocksLowerTriangular" | custom-call | tf_op jit(solution)/shard_map/triangular_solve | solution.py:11
  368.0 80.2 %all-reduce.6.cloned.1.call-done = f32[2048,256]{1,0:T(8,128)} async-done(((f32[2048,256]{1,0:T(8,128)}), f32[2048,256]{1,0:T(8,128)}) %all-reduce.6.cloned.1.call-update) | async-done | bytes 2097168 | tf_op jit(solution)/shard_map/psum | solution.py:100
  456.5 4.2 fusion.33
  461.2 40.8 %all-reduce.8.cloned.1.call-done = f32[256,256]{0,1:T(8,128)} async-done(((f32[256,256]{0,1:T(8,128)}), f32[256,256]{0,1:T(8,128)}) %all-reduce.8.cloned.1.call-update) | async-done | bytes 262160 | tf_op jit(solution)/shard_map/psum | solution.py:102
  507.1 195.0 %while.27 = (s32[]{:T(128)}, f32[64,8192]{1,0:T(8,128)S(1)}, s32[12,16]{1,0:T(8,128)}, f32[12,16]{1,0:T(8,128)}, bf16[12,16,32,1024]{3,2,1,0:T(8,128)(2,1)}, /*i...) while((s32[]{:T(128)}, f32[64,8192]{1,0:T(8,128)S(1)}, ...), condition=%wide.region_11.13_spmd.clone, body=%wide.region_10.12_spmd.clone.sunk | while | flops 378802272 | bytes 15213583 | solution.py:75
  508.4 4.4 reshape.345
  515.3 4.0 fusion.116
  524.7 4.4 reshape.345
  531.5 4.0 fusion.116
  540.9 4.4 reshape.345
  547.8 4.0 fusion.116
  557.2 4.4 reshape.345
  564.0 4.0 fusion.116
  573.4 4.4 reshape.345
  580.3 4.0 fusion.116
  589.7 4.4 reshape.345
  596.5 4.0 fusion.116
  605.9 4.4 reshape.345
  612.8 4.0 fusion.116
  622.2 4.4 reshape.345
  629.0 4.0 fusion.116
  638.4 4.4 reshape.345
  645.3 4.0 fusion.116
  654.7 4.4 reshape.345
  661.5 4.0 fusion.116
  670.9 4.4 reshape.345
  677.8 4.0 fusion.116
  687.2 4.4 reshape.345
  694.0 4.0 fusion.116
  706.2 11.7 %custom-call.32 = f32[128,128]{1,0:T(8,128)S(1)} custom-call(f32[128,128]{1,0:T(8,128)S(1)} %slice.104), custom_call_target="Cholesky" | custom-call | tf_op jit(solution)/shard_map/cholesky/custom-call.2 | solution.py:10
  718.0 9.8 %custom-call.33 = f32[1,128,128]{1,2,0:T(8,128)S(1)} custom-call(f32[1,128,128]{2,1,0:T(8,128)S(1)} %get-tuple-element.258), custom_call_target="InvertDiagBlocksLowerTriangular" | custom-call | tf_op jit(solution)/shard_map/cholesky/custom-call.7 | solution.py:10
  728.5 11.7 %custom-call.34 = f32[128,128]{1,0:T(8,128)S(1)} custom-call(f32[128,128]{1,0:T(8,128)S(1)} %convolution_subtract_fusion.4), custom_call_target="Cholesky" | custom-call | tf_op jit(solution)/shard_map/cholesky/custom-call.3 | solution.py:10
  742.9 4.0 while.25
  746.9 19.8 %custom-call.21 = f32[2,128,128]{1,2,0:T(8,128)S(1)} custom-call(f32[2,128,128]{2,1,0:T(8,128)S(1)} %get-tuple-element.124), custom_call_target="InvertDiagBlocksLowerTriangular" | custom-call | tf_op jit(solution)/shard_map/triangular_solve | solution.py:11
  (399 shorter events, 200.5 us)
Async XLA Ops:
  8.0 5.2 copy-start.5
  8.0 6.0 copy-start.8
  8.0 6.0 copy-start.12
  8.0 6.8 copy-start.13
  8.0 6.9 copy-start.14
  8.0 155.5 %all-reduce.10.cloned.1.call-start = ((), (), s32[]{:S(2)}) async-start(), calls=%async_computation.5 | async-start | bytes 1048576 | tf_op jit(solution)/shard_map/psum | solution.py:82
  13.2 185.7 %all-gather.2.cloned.1.call-start = ((), (), s32[]{:S(2)}) async-start(), calls=%async_computation.1 | async-start | bytes 1310720 | tf_op jit(solution)/shard_map/all_gather | solution.py:90
  14.0 434.3 %all-reduce.6.cloned.1.call-start = ((), (), s32[]{:S(2)}) async-start(), calls=%async_computation.2 | async-start | bytes 4194304 | tf_op jit(solution)/shard_map/psum | solution.py:100
  340.2 1.5 copy-start.10
  340.2 1.5 copy-start.11
  341.8 160.2 %all-reduce.8.cloned.1.call-start = ((), (), s32[]{:S(2)}) async-start(), calls=%async_computation.3 | async-start | bytes 524288 | tf_op jit(solution)/shard_map/psum | solution.py:102
  348.3 103.3 %copy-start.7 = (f32[256,256]{1,0:T(8,128)}, f32[256,256]{1,0:T(8,128)S(1)}, u32[]{:S(2)}) copy-start(f32[256,256]{1,0:T(8,128)S(1)} %get-tuple-element.553) | copy-start | bytes 786436
  348.3 103.3 %copy-start.15 = (s32[2,2]{1,0:T(2,128)}, s32[2,2]{1,0:T(2,128)S(1)}, u32[]{:S(2)}) copy-start(s32[2,2]{1,0:T(2,128)S(1)} %get-tuple-element.571) | copy-start | bytes 52
  448.3 2.4 copy-start.6
  453.6 51.0 %copy-start = (f32[2048,128]{1,0:T(8,128)}, f32[2048,128]{1,0:T(8,128)S(1)}, u32[]{:S(2)}) copy-start(f32[2048,128]{1,0:T(8,128)S(1)} %fusion.48) | copy-start | bytes 3145732
  456.5 4.7 copy-start.2
  460.7 306.1 %reduce-scatter.2.cloned.1.call-start = ((), (), s32[]{:S(2)}) async-start(), calls=%async_computation.4 | async-start | bytes 2621440 | tf_op jit(solution)/shard_map/reduce_scatter | solution.py:111
  703.6 1.2 copy-start.1
  703.6 1.5 copy-start.3
  703.6 2.2 copy-start.4
  703.6 2.2 copy-start.9
  706.0 36.9 %copy-start.16 = (s32[2,2]{1,0:T(2,128)S(1)}, s32[2,2]{1,0:T(2,128)}, u32[]{:S(2)}) copy-start(s32[2,2]{1,0:T(2,128)} %copy-done.15) | copy-start | bytes 52
Sparse Core Ops, SparseCore 0:
  13.8 149.6 all-reduce.9
Sparse Core Ops, SparseCore 1:
  15.9 26.6 all-gather.1
  341.9 106.3 all-reduce.5
  460.8 41.2 all-reduce.7
  703.7 30.0 reduce-scatter.1
where the time goes:
time: 792 us; the launch traced here: 780 us
  waiting for transfers between devices  257 us (32%)
  local copies, waits for them, and re-layouts  166 us (21%)
  other arithmetic  162 us (20%)
  matrix products  159 us (20%)
  between operations  19.7 us (2%)
  blocking collectives  13 us (2%)
    psum x1, waiting for transfers between devices, on_device(): lax.psum((jnp.dot(b_factor.T, b_factor, precision=highest), jnp.dot(c_fac...  136 us
    psum x1, waiting for transfers between devices, on_device(): whole_sum = lax.psum(partial_value, 'col')  80.2 us
    another operation x13, other arithmetic, solve_rows(): factor_low = lax.linalg.cholesky(gram)  68.6 us
    dot_general x24, matrix products, one_step(): jnp.dot(select, result.reshape(group_size, block_edge * rank_width), prec...  55 us
    reshape x12, local copies, waits for them, and re-layouts, one_step(): tensor_group.reshape(group_size, block_edge, block_edge, block_edge)  52.3 us
    dot_general x12, matrix products, one_step(): jnp.einsum('bijk,bikr->bjr', tensor_group.reshape(group_size, block_edge,...  48.5 us
    convert_element_type x12, other arithmetic, one_step(): (left_blk[:, :, None, :] * tail_blk[:, None, :, :]).astype(jnp.bfloat16)  46.2 us
    gather x24, local copies, waits for them, and re-layouts, one_step(): left_blk = left_table[left_idx].astype(jnp.float32)  42.9 us
  transfers between devices with their start and end apart: 5, of which 3 were waited for; matrix products, arithmetic and copies ran while one was open for 15% of the time, Pallas kernels for 0%

commit v1 on v0

--- a/solution.py
+++ b/solution.py
@@ -80,11 +80,14 @@
     highest = lax.Precision.HIGHEST
     block_edge = blocks.shape[1]
     gram_second, gram_third = lax.psum(
-        (
-            jnp.dot(b_factor.T, b_factor, precision=highest),
-            jnp.dot(c_factor.T, c_factor, precision=highest),
+        lax.psum(
+            (
+                jnp.dot(b_factor.T, b_factor, precision=highest),
+                jnp.dot(c_factor.T, c_factor, precision=highest),
+            ),
+            "grp",
         ),
-        ("grp", "col"),
+        "col",
     )
     b_range, c_range = (
         lax.all_gather(b_factor.astype(jnp.bfloat16), "grp", axis=0, tiled=True),

time: 792 us -> 711 us (0.90)
  waiting for transfers between devices: 257 us -> 161 us
  other arithmetic: 162 us -> 182 us
    psum x1, waiting for transfers between devices: 136 us -> 0.01 us  [on_device(): lax.psum((jnp.dot(b_factor.T, b_factor, precision=highest), jnp.dot(c_fac...]
    psum x1, waiting for transfers between devices: 80.2 us -> 110 us  [on_device(): whole_sum = lax.psum(partial_value, 'col')]
    all_gather x1, waiting for transfers between devices: 0.03 us -> 9.89 us  [on_device(): lax.all_gather(b_factor.astype(jnp.bfloat16), 'grp', axis=0, tiled=True)]
    convert_element_type x24, other arithmetic: 0.97 us -> 10.6 us  [one_step(): tail_blk = tail_table[tail_idx].astype(jnp.float32)]
    convert_element_type x24, other arithmetic: 0.97 us -> 10.6 us  [one_step(): left_blk = left_table[left_idx].astype(jnp.float32)]
  transfers between devices with their start and end apart: 5 -> 5, of which waited for: 3 -> 3; matrix products, arithmetic and copies ran while one was open for 15% -> 29% of each run, Pallas kernels for 0% -> 0%
where the time goes in v1:
time: 711 us; the launch traced here: 702 us
  other arithmetic  182 us (26%)
  local copies, waits for them, and re-layouts  167 us (23%)
  waiting for transfers between devices  161 us (23%)
  matrix products  158 us (22%)
  between operations  17.7 us (2%)
  blocking collectives  12.9 us (2%)
    psum x1, waiting for transfers between devices, on_device(): whole_sum = lax.psum(partial_value, 'col')  110 us
    another operation x13, other arithmetic, solve_rows(): factor_low = lax.linalg.cholesky(gram)  68.6 us
    dot_general x24, matrix products, one_step(): jnp.dot(select, result.reshape(group_size, block_edge * rank_width), prec...  54.9 us
    reshape x12, local copies, waits for them, and re-layouts, one_step(): tensor_group.reshape(group_size, block_edge, block_edge, block_edge)  52.3 us
    dot_general x12, matrix products, one_step(): jnp.einsum('bijk,bikr->bjr', tensor_group.reshape(group_size, block_edge,...  51.1 us
    convert_element_type x12, other arithmetic, one_step(): (left_blk[:, :, None, :] * tail_blk[:, None, :, :]).astype(jnp.bfloat16)  46.2 us
    gather x24, local copies, waits for them, and re-layouts, one_step(): left_blk = left_table[left_idx].astype(jnp.float32)  42.9 us
    psum x1, waiting for transfers between devices, on_device(): gram_first = lax.psum(jnp.dot(a_whole.T, a_whole, precision=highest), 'grp')  41.1 us
  transfers between devices with their start and end apart: 5, of which 3 were waited for; matrix products, arithmetic and copies ran while one was open for 29% of the time, Pallas kernels for 0%

profile of v1, /device:TPU:0, one launch (start us, length us, event | category | flops | bytes accessed | tf_op | source)
XLA Modules:
  0.0 701.8 jit_solution(14878679305588226521)
XLA Ops:
  13.1 12.9 %all_gather.7 = bf16[512,256]{1,0:T(8,128)(2,1)S(1)} all-gather(bf16[128,256]{1,0:T(8,128)(2,1)S(1)} %convert_element_type.56), channel_id=1, replica_groups=mesh['grp'=4,'col'=32] {'grp'}, dimensions={0}, use_global_device_ids=true | all-gather | bytes 327680 | tf_op jit(solution)/shard_map/all_gather | solution.py:94
  26.9 9.9 %all-gather.2.cloned.1.call-done = bf16[2048,256]{1,0:T(8,128)(2,1)} async-done(((bf16[512,256]{1,0:T(8,128)(2,1)}), bf16[2048,256]{1,0:T(8,128)(2,1)}) %all-gather.2.cloned.1.call-update) | async-done | bytes 1048592 | tf_op jit(solution)/shard_map/all_gather | solution.py:93
  36.8 141.0 %while.26 = (s32[]{:T(128)}, f32[64,8192]{1,0:T(8,128)S(1)}, s32[12,16]{1,0:T(8,128)S(1)}, f32[12,16]{1,0:T(8,128)S(1)}, bf16[12,16,32,1024]{3,2,1,0:T(8,128)(2,...) while((s32[]{:T(128)}, f32[64,8192]{1,0:T(8,128)S(1)}, ...), condition=%wide.region_1.0_spmd.clone, body=%wide.region_0.0_spmd.clone.sunk | while | flops 378802272 | bytes 27796992 | solution.py:75
  39.3 3.9 multiply_convert_fusion.5
  51.0 3.9 multiply_convert_fusion.5
  54.9 2.7 fusion.109
  62.8 3.9 multiply_convert_fusion.5
  66.6 2.7 fusion.109
  74.5 3.9 multiply_convert_fusion.5
  78.4 2.7 fusion.109
  86.3 3.9 multiply_convert_fusion.5
  90.2 2.7 fusion.109
  98.1 3.9 multiply_convert_fusion.5
  101.9 2.7 fusion.109
  109.8 3.9 multiply_convert_fusion.5
  113.7 2.7 fusion.109
  121.6 3.9 multiply_convert_fusion.5
  125.4 2.7 fusion.109
  133.3 3.9 multiply_convert_fusion.5
  137.2 2.7 fusion.109
  145.1 3.9 multiply_convert_fusion.5
  148.9 2.7 fusion.109
  156.8 3.9 multiply_convert_fusion.5
  160.7 2.7 fusion.109
  168.6 3.9 multiply_convert_fusion.5
  172.4 2.7 fusion.109
  179.6 109.8 %all-reduce.9.cloned.1.call-done = (f32[2048,256]{1,0:T(8,128)}, f32[256,256]{0,1:T(8,128)}, f32[256,256]{0,1:T(8,128)}) async-done(((f32[2048,256]{1,0:T(8,128)}, f32[256,256]{0,1:T(8,128)}, f32[256,256]{0,1:T(8,128)}), (f32[2048,256]{1,0:T(8,128)}, f32[256,256]{0,1:T(8,128)}, f32[256,256]{0,1:T(8,128)})) %all-reduce.9.cloned.1.call-update) | async-done | bytes 2621456 | tf_op jit(solution)/shard_map/psum | solution.py:103
  290.8 11.7 %custom-call.29 = f32[128,128]{1,0:T(8,128)S(1)} custom-call(f32[128,128]{1,0:T(8,128)S(1)} %slice.101), custom_call_target="Cholesky" | custom-call | tf_op jit(solution)/shard_map/cholesky/custom-call.2 | solution.py:10
  302.5 9.8 %custom-call.30 = f32[1,128,128]{1,2,0:T(8,128)S(1)} custom-call(f32[1,128,128]{2,1,0:T(8,128)S(1)} %get-tuple-element.265), custom_call_target="InvertDiagBlocksLowerTriangular" | custom-call | tf_op jit(solution)/shard_map/cholesky/custom-call.7 | solution.py:10
  313.0 11.7 %custom-call.31 = f32[128,128]{1,0:T(8,128)S(1)} custom-call(f32[128,128]{1,0:T(8,128)S(1)} %convolution_subtract_fusion.5), custom_call_target="Cholesky" | custom-call | tf_op jit(solution)/shard_map/cholesky/custom-call.3 | solution.py:10
  326.9 4.5 while.24
  331.3 19.7 %custom-call.20 = f32[2,128,128]{1,2,0:T(8,128)S(1)} custom-call(f32[2,128,128]{2,1,0:T(8,128)S(1)} %get-tuple-element.116), custom_call_target="InvertDiagBlocksLowerTriangular" | custom-call | tf_op jit(solution)/shard_map/triangular_solve | solution.py:11
  357.9 4.2 fusion.33
  362.4 41.1 %all-reduce.7.cloned.1.call-done = f32[256,256]{0,1:T(8,128)} async-done(((f32[256,256]{0,1:T(8,128)}), f32[256,256]{0,1:T(8,128)}) %all-reduce.7.cloned.1.call-update) | async-done | bytes 262160 | tf_op jit(solution)/shard_map/psum | solution.py:105
  408.7 216.4 %while.27 = (s32[]{:T(128)}, f32[64,8192]{1,0:T(8,128)S(1)}, s32[12,16]{1,0:T(8,128)}, f32[12,16]{1,0:T(8,128)}, bf16[12,16,32,1024]{3,2,1,0:T(8,128)(2,1)}, /*i...) while((s32[]{:T(128)}, f32[64,8192]{1,0:T(8,128)S(1)}, ...), condition=%wide.region_13.15_spmd.clone, body=%wide.region_12.14_spmd.clone.sunk | while | flops 378802272 | bytes 15213575 | solution.py:75
  414.1 4.4 reshape.345
  418.4 4.3 fusion.116
  432.1 4.4 reshape.345
  436.5 4.3 fusion.116
  450.1 4.4 reshape.345
  454.5 4.3 fusion.116
  468.2 4.4 reshape.345
  472.5 4.3 fusion.116
  486.2 4.4 reshape.345
  490.5 4.3 fusion.116
  504.2 4.4 reshape.345
  508.6 4.3 fusion.116
  522.2 4.4 reshape.345
  526.6 4.3 fusion.116
  540.3 4.4 reshape.345
  544.6 4.3 fusion.116
  558.3 4.4 reshape.345
  562.7 4.3 fusion.116
  576.3 4.4 reshape.345
  580.7 4.3 fusion.116
  594.4 4.4 reshape.345
  598.8 4.3 fusion.116
  612.4 4.4 reshape.345
  616.8 4.3 fusion.116
  629.2 11.7 %custom-call.32 = f32[128,128]{1,0:T(8,128)S(1)} custom-call(f32[128,128]{1,0:T(8,128)S(1)} %slice.104), custom_call_target="Cholesky" | custom-call | tf_op jit(solution)/shard_map/cholesky/custom-call.2 | solution.py:10
  641.0 9.8 %custom-call.33 = f32[1,128,128]{1,2,0:T(8,128)S(1)} custom-call(f32[1,128,128]{2,1,0:T(8,128)S(1)} %get-tuple-element.261), custom_call_target="InvertDiagBlocksLowerTriangular" | custom-call | tf_op jit(solution)/shard_map/cholesky/custom-call.7 | solution.py:10
  651.5 11.7 %custom-call.34 = f32[128,128]{1,0:T(8,128)S(1)} custom-call(f32[128,128]{1,0:T(8,128)S(1)} %convolution_subtract_fusion.4), custom_call_target="Cholesky" | custom-call | tf_op jit(solution)/shard_map/cholesky/custom-call.3 | solution.py:10
  665.8 3.8 while.25
  669.7 19.9 %custom-call.21 = f32[2,128,128]{1,2,0:T(8,128)S(1)} custom-call(f32[2,128,128]{2,1,0:T(8,128)S(1)} %get-tuple-element.124), custom_call_target="InvertDiagBlocksLowerTriangular" | custom-call | tf_op jit(solution)/shard_map/triangular_solve | solution.py:11
  (397 shorter events, 218.0 us)
Async XLA Ops:
  7.2 4.1 copy-start.5
  7.2 5.9 copy-start.7
  7.2 19.4 %copy-start.11 = (s32[192]{0:T(256)S(1)}, s32[192]{0:T(256)}, u32[]{:S(2)}) copy-start(s32[192]{0:T(256)} %param.13) | copy-start | bytes 2308
  7.2 19.5 %copy-start.12 = (s32[192]{0:T(256)S(1)}, s32[192]{0:T(256)}, u32[]{:S(2)}) copy-start(s32[192]{0:T(256)} %param.14) | copy-start | bytes 2308
  7.2 19.6 %copy-start.13 = (s32[192]{0:T(256)S(1)}, s32[192]{0:T(256)}, u32[]{:S(2)}) copy-start(s32[192]{0:T(256)} %param.15) | copy-start | bytes 2308
  7.2 29.6 %all-gather.2.cloned.1.call-start = ((), (), s32[]{:S(2)}) async-start(), calls=%async_computation.1 | async-start | bytes 1310720 | tf_op jit(solution)/shard_map/all_gather | solution.py:93
  9.1 170.3 %all-reduce.11.cloned.1.call-start = ((), (), s32[]{:S(2)}) async-start(), calls=%async_computation.5 | async-start | bytes 1048576 | tf_op jit(solution)/shard_map/psum | solution.py:83
  13.0 276.5 %all-reduce.9.cloned.1.call-start = ((), (), s32[]{:S(2)}) async-start(), calls=%async_computation.4 | async-start | bytes 5242880 | tf_op jit(solution)/shard_map/psum | solution.py:103
  177.8 1.5 copy-start.9
  177.8 1.5 copy-start.10
  179.4 224.2 %all-reduce.7.cloned.1.call-start = ((), (), s32[]{:S(2)}) async-start(), calls=%async_computation.2 | async-start | bytes 524288 | tf_op jit(solution)/shard_map/psum | solution.py:105
  290.6 60.5 %copy-start.6 = (f32[2048,256]{1,0:T(8,128)S(1)}, f32[2048,256]{1,0:T(8,128)}, u32[]{:S(2)}) copy-start(f32[2048,256]{1,0:T(8,128)} %get-tuple-element.245) | copy-start | bytes 6291460
  331.3 21.7 %copy-start.14 = (s32[2,2]{1,0:T(2,128)}, s32[2,2]{1,0:T(2,128)S(1)}, u32[]{:S(2)}) copy-start(s32[2,2]{1,0:T(2,128)S(1)} %get-tuple-element.584) | copy-start | bytes 52
  355.0 51.2 %copy-start = (f32[2048,128]{1,0:T(8,128)}, f32[2048,128]{1,0:T(8,128)S(1)}, u32[]{:S(2)}) copy-start(f32[2048,128]{1,0:T(8,128)S(1)} %fusion.48) | copy-start | bytes 3145732
  357.0 1.0 copy-start.2
  362.2 327.4 %reduce-scatter.2.cloned.1.call-start = ((), (), s32[]{:S(2)}) async-start(), calls=%async_computation.3 | async-start | bytes 2621440 | tf_op jit(solution)/shard_map/reduce_scatter | solution.py:114
  626.6 1.2 copy-start.1
  626.6 1.5 copy-start.3
  626.6 2.2 copy-start.4
  626.6 2.2 copy-start.8
  629.0 36.8 %copy-start.15 = (s32[2,2]{1,0:T(2,128)S(1)}, s32[2,2]{1,0:T(2,128)}, u32[]{:S(2)}) copy-start(s32[2,2]{1,0:T(2,128)} %copy-done.14) | copy-start | bytes 52
Sparse Core Ops, SparseCore 0:
  10.3 26.4 all-gather.1
  39.2 43.8 all-reduce.10
  179.5 109.9 all-reduce.8
  362.3 41.2 all-reduce.6
  626.7 30.1 reduce-scatter.1
